TPU v7x, 32 devices: a whole 2x2x4 slice. The times are simulated.
32 devices in a mesh: groups: 2 (over x), col: 16 (over z, y, core).
Axes of the slice: x: 2, y: 2, z: 4, core: 2. Of those that a mesh axis runs over, the one named last changes fastest.
Arguments:
- slab: float32 [2, 2048, 4096], P(None, 'groups', 'col'), parts along dimension 1, may hold values from -6 to 6
- block_on: int32 [16, 32], P('groups', 'col'), parts along dimension 0, may hold values 0 or 1
- block_band: int32 [16, 32], P('groups', 'col'), parts along dimension 0, may hold values from 0 to 3
- band_gain: float32 [4], replicated, may hold values from 0.25 to 2
Outputs:
- spectra: float32 [2, 2048, 4096], P(None, 'groups', 'col'), parts along dimension 1
There are 2 independent parts, one for each index of `groups`. A program takes and returns all parts, laid end to end along the dimension named above; an argument that names none is the same for every part. Nothing has to cross between parts.
All inputs are finite; a program needn't handle non-finite values. No bound on the sum of `block_on` on one device may be relied on, other than what follows from the above.
Results may differ from a plain program's by a relative error of at most 0.00007.
Values sent between devices are 32-bit elements; how exact they have to be, the bound alone decides.
No kernel may reach another device: no remote copies, remote signals or barrier semaphores. Data moves between devices by JAX's collectives and lax.ppermute only.
A program may use at most 64 MiB of HBM per device.

v0:
```python
import math
import jax
import jax.numpy as jnp
from jax import lax
from jax.sharding import PartitionSpec as P

BLOCK = 128


def phase_table(first_index, second_index, length):
    product = first_index[:, None] * second_index[None, :] % length
    angles = product.astype(jnp.float32) * (2.0 * math.pi / length)
    return (jnp.cos(angles), -jnp.sin(angles))


def contract(stacked, table, formula):
    cosine_table, sine_table = table
    real_part = jnp.einsum(
        formula, stacked[0], cosine_table, precision=lax.Precision.HIGHEST
    ) - jnp.einsum(formula, stacked[1], sine_table, precision=lax.Precision.HIGHEST)
    imag_part = jnp.einsum(
        formula, stacked[0], sine_table, precision=lax.Precision.HIGHEST
    ) + jnp.einsum(formula, stacked[1], cosine_table, precision=lax.Precision.HIGHEST)
    return jnp.stack([real_part, imag_part])


def rotate(stacked, table):
    cosine_table, sine_table = table
    real_part = stacked[0] * cosine_table - stacked[1] * sine_table
    imag_part = stacked[0] * sine_table + stacked[1] * cosine_table
    return jnp.stack([real_part, imag_part])


def shards(slab, block_on, block_band, band_gain):
    devices = lax.axis_size("col")
    rows_total = slab.shape[1]
    shard_cols = slab.shape[2]
    length = shard_cols * devices
    rows_here = rows_total // devices
    factor = 1.0 / math.sqrt(length)
    first_len = BLOCK
    second_len = length // first_len
    first_iota = jnp.arange(first_len, dtype=jnp.int32)
    second_iota = jnp.arange(second_len, dtype=jnp.int32)
    table_one = phase_table(first_iota, first_iota, first_len)
    table_middle = phase_table(first_iota, second_iota, length)
    table_two = phase_table(second_iota, second_iota, second_len)
    received = lax.all_to_all(
        slab.reshape(2, devices, rows_here, shard_cols),
        "col",
        split_axis=1,
        concat_axis=3,
        tiled=True,
    )
    row_count = received.shape[2]
    square = received[:, 0].reshape(2, row_count, first_len, second_len)
    mixture = contract(square, table_one, "rab,ak->rkb")
    mixture = rotate(mixture, table_middle)
    result = contract(mixture, table_two, "rkb,bm->rmk")
    whole = result.reshape(2, 1, row_count, length)
    whole = whole.reshape(2, rows_here, devices, shard_cols)
    spectrum = lax.all_to_all(whole, "col", split_axis=2, concat_axis=1, tiled=True).reshape(
        2, rows_total, shard_cols
    )
    choose = (block_band[..., None] == jnp.arange(band_gain.shape[0], dtype=jnp.int32)).astype(
        jnp.float32
    )
    weight = block_on.astype(jnp.float32) * jnp.sum(choose * band_gain, axis=-1) * factor
    row_blocks = rows_total // BLOCK
    col_blocks = shard_cols // BLOCK
    masked = (
        spectrum.reshape(2, row_blocks, BLOCK, col_blocks, BLOCK) * weight[None, :, None, :, None]
    )
    return masked.reshape(2, rows_total, shard_cols)


def solution(mesh):
    placed = (P(None, "groups", "col"), P("groups", "col"), P("groups", "col"), P())
    return jax.shard_map(
        shards, mesh=mesh, in_specs=placed, out_specs=P(None, "groups", "col"), check_vma=False
    )
```

profile of v0, /device:TPU:13, one launch (start us, length us, event | category | flops | bytes accessed | tf_op | source)
XLA Modules:
  0.0 138.4 jit_solution(2403043482625478237)
XLA Ops:
  0.0 3.1 %copy.54 = f32[2,16,64,256]{3,2,0,1:T(8,128)} copy(f32[2,16,64,256]{3,2,1,0:T(8,128)} %bitcast.56) | data formatting | bytes 4194304 | tf_op jit(solution)/shard_map/reshape | solution.py:49
  3.1 6.5 %all-to-all-start = ((f32[2,16,64,256]{3,2,0,1:T(8,128)}), f32[2,16,64,256]{3,2,0,1:T(8,128)S(1)}, u32[]{:S(2)}, u32[]{:S(2)}) async-start(f32[2,16,64,256]{3,2,0,1:T(8,128)} %copy.54), calls=%async_computation | async-start | bytes 4194304 | tf_op jit(solution)/shard_map/all_to_all | solution.py:48
  9.7 0.1 sine_negate_fusion.4
  9.7 47.3 %all-to-all-done = f32[2,16,64,256]{3,2,0,1:T(8,128)S(1)} async-done(((f32[2,16,64,256]{3,2,0,1:T(8,128)}), f32[2,16,64,256]{3,2,0,1:T(8,128)S(1)}, u32[]{:S(2)}, u32[]{:S(2)}) %all-to-all-start) | async-done | bytes 2097184 | tf_op jit(solution)/shard_map/all_to_all | solution.py:48
  57.1 1.2 fusion.79
  58.2 0.6 copy.55
  58.8 1.3 copy.56
  60.1 0.0 copy-start.1
  60.1 1.2 fusion.11
  61.4 2.2 %fusion.15 = f32[128,64,32]{0,1,2:T(8,128)} fusion(f32[64,128,32]{1,0,2:T(8,128)S(1)} %copy.56), kind=kOutput, calls=%fused_computation.27 | convolution fusion | flops 402882560 | bytes 2097152 | tf_op jit(solution)/shard_map/rab,ak->rkb/dot_general | solution.py:18
  63.6 0.0 copy-done.1
  63.6 1.9 %copy.57 = f32[1,1,64,16,256]{2,4,3,1,0:T(8,128)} copy(f32[1,1,64,16,256]{4,2,0,3,1:T(8,128)S(1)} %copy-done.1) | data formatting | bytes 2097152 | tf_op jit(solution)/shard_map/slice | solution.py:20
  65.5 2.7 %copy.58 = f32[64,128,32]{1,0,2:T(8,128)S(1)} copy(f32[64,128,32]{0,2,1:T(8,128)} %bitcast.52) | data formatting | bytes 2097152 | tf_op jit(solution)/shard_map/squeeze | solution.py:20
  68.2 0.0 copy-start
  68.2 1.3 convolution_add_fusion.1
  69.5 0.0 copy-done
  69.5 1.4 %add_bitcast_fusion = (f32[64,128,32]{1,0,2:T(8,128)S(1)}, f32[64,128,32]{1,0,2:T(8,128)S(1)}) fusion(f32[128,64,32]{0,1,2:T(8,128)S(1)} %convolution_add_fusion.1, f32[128,32]{0,1:T(8,128)S(1)} %get-tuple-element.9, f32[128,32]{0,1:T(8,128)S(1)} %get-tuple-element.10, f32[128,64,32]{0,1,2:T(8,128)S(1)} %copy-done, f32[64,128,32]{1,0,2:T(8,128)S(1)} %copy.58), kind=kOutput, calls=%fused_computation.9 | convolution fusion | flops 404733952 | bytes 5275648 | tf_op jit(solution)/shard_map/rab,ak->rkb/dot_general | solution.py:20
  70.9 1.6 %fusion.6 = f32[32,64,128]{2,0,1:T(8,128)S(1)} fusion(f32[64,128,32]{1,0,2:T(8,128)S(1)} %get-tuple-element.6), kind=kOutput, calls=%fused_computation.15 | convolution fusion | flops 100677632 | bytes 2097152 | tf_op jit(solution)/shard_map/rkb,bm->rmk/dot_general | solution.py:18
  72.5 1.6 %fusion.4 = f32[32,64,128]{2,0,1:T(8,128)S(1)} fusion(f32[64,128,32]{1,0,2:T(8,128)S(1)} %get-tuple-element.6), kind=kOutput, calls=%fused_computation.13 | convolution fusion | flops 100678656 | bytes 2097152 | tf_op jit(solution)/shard_map/rkb,bm->rmk/dot_general | solution.py:21
  74.1 1.8 %fusion.1 = f32[64,32,128]{2,1,0:T(8,128)S(1)} fusion(f32[32,64,128]{2,0,1:T(8,128)S(1)} %fusion.6, f32[64,128,32]{1,0,2:T(8,128)S(1)} %get-tuple-element.5), kind=kOutput, calls=%fused_computation.5 | convolution fusion | flops 100940800 | bytes 3145728 | tf_op jit(solution)/shard_map/rkb,bm->rmk/dot_general | solution.py:20
  75.9 1.3 stack.9
  77.1 2.8 %copy.65 = f32[1,64,16,256]{3,1,0,2:T(8,128)} copy(f32[1,64,16,256]{3,2,1,0:T(8,128)} %stack.9) | data formatting | bytes 2097152 | tf_op jit(solution)/shard_map/stack | solution.py:24
  79.9 1.6 %fusion = f32[64,32,128]{2,1,0:T(8,128)S(1)} fusion(f32[32,64,128]{2,0,1:T(8,128)S(1)} %fusion.4, f32[64,128,32]{1,0,2:T(8,128)S(1)} %get-tuple-element.5), kind=kOutput, calls=%fused_computation.3 | convolution fusion | flops 100939776 | bytes 3145728 | tf_op jit(solution)/shard_map/rkb,bm->rmk/dot_general | solution.py:23
  81.5 0.0 copy-start.2
  81.6 0.3 stack.10
  81.9 0.6 copy.66
  82.5 0.3 copy-done.2
  82.8 1.5 %pad_maximum_fusion = f32[2,64,16,256]{3,1,0,2:T(8,128)} fusion(f32[1,64,16,256]{3,1,0,2:T(8,128)S(1)} %copy.66, f32[1,64,16,256]{3,1,0,2:T(8,128)S(1)} %copy-done.2), kind=kLoop, calls=%fused_computation | loop fusion | flops 524288 | bytes 4194304 | tf_op jit(solution)/shard_map/stack | solution.py:24
  84.2 0.0 copy-start.4
  84.2 0.0 copy-start.5
  84.2 0.0 copy-start.3
  84.2 4.9 %all-to-all-start.1 = ((f32[2,64,16,256]{3,1,0,2:T(8,128)}), f32[2,64,16,256]{3,1,0,2:T(8,128)S(1)}, u32[]{:S(2)}, u32[]{:S(2)}) async-start(f32[2,64,16,256]{3,1,0,2:T(8,128)} %pad_maximum_fusion), calls=%async_computation.1 | async-start | bytes 4194304 | tf_op jit(solution)/shard_map/all_to_all | solution.py:62
  89.2 0.0 copy-done.4
  89.2 0.0 copy-done.5
  89.2 0.1 select_reduce_fusion
  89.3 0.0 copy-done.3
  89.3 0.1 copy.68
  89.4 0.3 mul.231
  89.7 0.1 copy.79
  89.8 46.8 %all-to-all-done.1 = f32[2,64,16,256]{3,1,0,2:T(8,128)S(1)} async-done(((f32[2,64,16,256]{3,1,0,2:T(8,128)}), f32[2,64,16,256]{3,1,0,2:T(8,128)S(1)}, u32[]{:S(2)}, u32[]{:S(2)}) %all-to-all-start.1) | async-done | bytes 2097184 | tf_op jit(solution)/shard_map/all_to_all | solution.py:62
  136.6 0.2 copy.67
  136.8 1.5 %bitcast_multiply_fusion = f32[2,1024,256]{2,1,0:T(8,128)} fusion(f32[2,64,16,256]{3,1,2,0:T(8,128)S(1)} %copy.67, f32[1024,256]{1,0:T(8,128)S(1)} %bitcast.54), kind=kLoop, calls=%fused_computation.1 | loop fusion | flops 524288 | bytes 5242880 | tf_op jit(solution)/shard_map/mul | solution.py:72
  (1 shorter events, 0.0 us)
Async XLA Ops:
  3.1 53.9 %all-to-all-start = ((f32[2,16,64,256]{3,2,0,1:T(8,128)}), f32[2,16,64,256]{3,2,0,1:T(8,128)S(1)}, u32[]{:S(2)}, u32[]{:S(2)}) async-start(f32[2,16,64,256]{3,2,0,1:T(8,128)} %copy.54), calls=%async_computation | async-start | bytes 4194304 | tf_op jit(solution)/shard_map/all_to_all | solution.py:48
  60.1 3.5 %copy-start.1 = (f32[1,1,64,16,256]{4,2,0,3,1:T(8,128)S(1)}, f32[1,1,64,16,256]{4,2,0,3,1:T(8,128)}, u32[]{:S(2)}) copy-start(f32[1,1,64,16,256]{4,2,0,3,1:T(8,128)} %get-tuple-element.7) | copy-start | bytes 3145732
  68.2 1.3 copy-start
  81.5 1.2 copy-start.2
  84.2 5.0 %copy-start.4 = (s32[8,2]{0,1:T(2,128)S(1)}, s32[8,2]{0,1:T(2,128)}, u32[]{:S(2)}) copy-start(s32[8,2]{0,1:T(2,128)} %param.6) | copy-start | bytes 196
  84.2 5.0 %copy-start.5 = (f32[4]{0:T(128)S(1)}, f32[4]{0:T(128)}, u32[]{:S(2)}) copy-start(f32[4]{0:T(128)} %param.7) | copy-start | bytes 52
  84.2 5.0 %copy-start.3 = (s32[8,2]{0,1:T(2,128)S(1)}, s32[8,2]{0,1:T(2,128)}, u32[]{:S(2)}) copy-start(s32[8,2]{0,1:T(2,128)} %param.5) | copy-start | bytes 196
  84.2 52.4 %all-to-all-start.1 = ((f32[2,64,16,256]{3,1,0,2:T(8,128)}), f32[2,64,16,256]{3,1,0,2:T(8,128)S(1)}, u32[]{:S(2)}, u32[]{:S(2)}) async-start(f32[2,64,16,256]{3,1,0,2:T(8,128)} %pad_maximum_fusion), calls=%async_computation.1 | async-start | bytes 4194304 | tf_op jit(solution)/shard_map/all_to_all | solution.py:62
where the time goes:
time: 139 us; the launch traced here: 138 us
  waiting for transfers between devices  94.1 us (68%)
  local copies, waits for them, and re-layouts  16.8 us (12%)
  matrix products  12.7 us (9%)
  starting transfers between devices  11.5 us (8%)
  other arithmetic  3.18 us (2%)
    all_to_all x1, waiting for transfers between devices, shards(): lax.all_to_all(slab.reshape(2, devices, rows_here, shard_cols), 'col', sp...  47.3 us
    all_to_all x1, waiting for transfers between devices, shards(): lax.all_to_all(whole, 'col', split_axis=2, concat_axis=1, tiled=True)  46.8 us
    all_to_all x1, starting transfers between devices, shards(): lax.all_to_all(slab.reshape(2, devices, rows_here, shard_cols), 'col', sp...  6.52 us
    another operation x4, local copies, waits for them, and re-layouts, contract(): return jnp.stack([real_part, imag_part])  4.98 us
    all_to_all x1, starting transfers between devices, shards(): lax.all_to_all(whole, 'col', split_axis=2, concat_axis=1, tiled=True)  4.94 us
    dot_general x2, matrix products, contract(): jnp.einsum(formula, stacked[0], cosine_table, precision=lax.Precision.HIG...  3.8 us
    dot_general x2, matrix products, contract(): jnp.einsum(formula, stacked[1], sine_table, precision=lax.Precision.HIGHEST)  3.18 us
    reshape x1, local copies, waits for them, and re-layouts, shards(): slab.reshape(2, devices, rows_here, shard_cols)  3.13 us
  transfers between devices with their start and end apart: 2, of which 2 were waited for; matrix products, arithmetic and copies ran while one was open for 0% of the time, Pallas kernels for 0%

commit v1 on v0

--- a/solution.py
+++ b/solution.py
@@ -5,6 +5,22 @@
 from jax.sharding import PartitionSpec as P
 
 BLOCK = 128
+
+
+def pairwise_exchange(array, axis, split, join):
+    ways, here = (lax.axis_size(axis), lax.axis_index(axis))
+    width = array.shape[split] // ways
+    lengths = list(array.shape)
+    lengths[split] = width
+    height = lengths[join]
+    lengths[join] = height * ways
+    full = jnp.zeros(lengths, array.dtype)
+    for mask in range(ways):
+        part = lax.dynamic_slice_in_dim(array, (here ^ mask) * width, width, axis=split)
+        if mask:
+            part = lax.ppermute(part, axis, [(d, d ^ mask) for d in range(ways)])
+        full = lax.dynamic_update_slice_in_dim(full, part, (here ^ mask) * height, axis=join)
+    return full
 
 
 def phase_table(first_index, second_index, length):
@@ -59,9 +75,7 @@
     result = contract(mixture, table_two, "rkb,bm->rmk")
     whole = result.reshape(2, 1, row_count, length)
     whole = whole.reshape(2, rows_here, devices, shard_cols)
-    spectrum = lax.all_to_all(whole, "col", split_axis=2, concat_axis=1, tiled=True).reshape(
-        2, rows_total, shard_cols
-    )
+    spectrum = pairwise_exchange(whole, "col", 2, 1).reshape(2, rows_total, shard_cols)
     choose = (block_band[..., None] == jnp.arange(band_gain.shape[0], dtype=jnp.int32)).astype(
         jnp.float32
     )

time: 139 us -> 146 us (1.050)
  starting transfers between devices: 11.5 us -> 23 us
  waiting for transfers between devices: 94.1 us -> 85.9 us
  local copies, waits for them, and re-layouts: 16.8 us -> 19.1 us
  matrix products: 12.7 us -> 14.6 us
  other arithmetic: 3.18 us -> 1.7 us
    all_to_all x1 -> x0, waiting for transfers between devices: 46.8 us -> none  [shards(): lax.all_to_all(whole, 'col', split_axis=2, concat_axis=1, tiled=True)]
    ppermute x0 -> x15, waiting for transfers between devices: none -> 38.7 us  [pairwise_exchange(): part = lax.ppermute(part, axis, [(d, d ^ mask) for d in range(ways)])]
    ppermute x0 -> x15, starting transfers between devices: none -> 16.3 us  [pairwise_exchange(): part = lax.ppermute(part, axis, [(d, d ^ mask) for d in range(ways)])]
    all_to_all x1 -> x0, starting transfers between devices: 4.94 us -> none  [shards(): lax.all_to_all(whole, 'col', split_axis=2, concat_axis=1, tiled=True)]
    unnamed x13 -> x28, local copies, waits for them, and re-layouts: 0.39 us -> 2.05 us
    another operation x4 -> x3, local copies, waits for them, and re-layouts: 4.98 us -> 3.41 us  [contract(): return jnp.stack([real_part, imag_part])]
    another operation x1 -> x0, other arithmetic: 1.47 us -> none  [contract(): return jnp.stack([real_part, imag_part])]
  transfers between devices with their start and end apart: 2 -> 16, of which waited for: 2 -> 11; matrix products, arithmetic and copies ran while one was open for 0% -> 1% of each run, Pallas kernels for 0% -> 0%
where the time goes in v1:
time: 146 us; the launch traced here: 145 us
  waiting for transfers between devices  85.9 us (59%)
  starting transfers between devices  23 us (16%)
  local copies, waits for them, and re-layouts  19.1 us (13%)
  matrix products  14.6 us (10%)
  other arithmetic  1.7 us (1%)
    all_to_all x1, waiting for transfers between devices, shards(): lax.all_to_all(slab.reshape(2, devices, rows_here, shard_cols), 'col', sp...  47.2 us
    ppermute x15, waiting for transfers between devices, pairwise_exchange(): part = lax.ppermute(part, axis, [(d, d ^ mask) for d in range(ways)])  38.7 us
    ppermute x15, starting transfers between devices, pairwise_exchange(): part = lax.ppermute(part, axis, [(d, d ^ mask) for d in range(ways)])  16.3 us
    all_to_all x1, starting transfers between devices, shards(): lax.all_to_all(slab.reshape(2, devices, rows_here, shard_cols), 'col', sp...  6.65 us
    dot_general x2, matrix products, contract(): jnp.einsum(formula, stacked[1], cosine_table, precision=lax.Precision.HIG...  3.84 us
    dot_general x2, matrix products, contract(): jnp.einsum(formula, stacked[0], sine_table, precision=lax.Precision.HIGHEST)  3.82 us
    dot_general x2, matrix products, contract(): jnp.einsum(formula, stacked[0], cosine_table, precision=lax.Precision.HIG...  3.81 us
    another operation x3, local copies, waits for them, and re-layouts, contract(): return jnp.stack([real_part, imag_part])  3.41 us
  transfers between devices with their start and end apart: 16, of which 11 were waited for; matrix products, arithmetic and copies ran while one was open for 1% of the time, Pallas kernels for 0%

profile of v1, /device:TPU:13, one launch (start us, length us, event | category | flops | bytes accessed | tf_op | source)
XLA Modules:
  0.0 144.8 jit_solution(14577145780720802206)
XLA Ops:
  0.0 3.1 %copy.55 = f32[2,16,64,256]{3,2,0,1:T(8,128)} copy(f32[2,16,64,256]{3,2,1,0:T(8,128)} %bitcast.82) | data formatting | bytes 4194304 | tf_op jit(solution)/shard_map/reshape | solution.py:65
  3.1 6.7 %all-to-all-start = ((f32[2,16,64,256]{3,2,0,1:T(8,128)}), f32[2,16,64,256]{3,2,0,1:T(8,128)S(1)}, u32[]{:S(2)}, u32[]{:S(2)}) async-start(f32[2,16,64,256]{3,2,0,1:T(8,128)} %copy.55), calls=%async_computation | async-start | bytes 4194304 | tf_op jit(solution)/shard_map/all_to_all | solution.py:64
  9.8 0.1 sine_negate_fusion.4
  9.9 0.0 copy-done.11
  9.9 0.1 select_reduce_fusion
  10.0 47.2 %all-to-all-done = f32[2,16,64,256]{3,2,0,1:T(8,128)S(1)} async-done(((f32[2,16,64,256]{3,2,0,1:T(8,128)}), f32[2,16,64,256]{3,2,0,1:T(8,128)S(1)}, u32[]{:S(2)}, u32[]{:S(2)}) %all-to-all-start) | async-done | bytes 2097184 | tf_op jit(solution)/shard_map/all_to_all | solution.py:64
  57.2 1.2 fusion.79
  58.4 0.6 copy.56
  59.0 1.3 copy.57
  60.3 1.2 fusion.11
  61.5 2.2 %fusion.15 = f32[128,64,32]{0,1,2:T(8,128)} fusion(f32[64,128,32]{1,0,2:T(8,128)S(1)} %copy.57), kind=kOutput, calls=%fused_computation.44 | convolution fusion | flops 402882560 | bytes 2097152 | tf_op jit(solution)/shard_map/rab,ak->rkb/dot_general | solution.py:34
  63.7 1.9 %copy.58 = f32[1,1,64,16,256]{2,4,3,1,0:T(8,128)} copy(f32[1,1,64,16,256]{4,2,0,3,1:T(8,128)S(1)} %copy-done.2) | data formatting | bytes 2097152 | tf_op jit(solution)/shard_map/slice | solution.py:36
  65.7 2.7 %copy.59 = f32[64,128,32]{1,0,2:T(8,128)S(1)} copy(f32[64,128,32]{0,2,1:T(8,128)} %bitcast.78) | data formatting | bytes 2097152 | tf_op jit(solution)/shard_map/squeeze | solution.py:36
  68.3 1.3 convolution_add_fusion.1
  69.6 1.4 add_bitcast_fusion
  71.0 1.6 %fusion.6 = f32[32,64,128]{2,0,1:T(8,128)S(1)} fusion(f32[64,128,32]{1,0,2:T(8,128)S(1)} %get-tuple-element.6), kind=kOutput, calls=%fused_computation.16 | convolution fusion | flops 100677632 | bytes 2097152 | tf_op jit(solution)/shard_map/rkb,bm->rmk/dot_general | solution.py:34
  72.7 2.6 %fusion.4 = f32[32,64,128]{2,0,1:T(8,128)} fusion(f32[64,128,32]{1,0,2:T(8,128)S(1)} %get-tuple-element.6), kind=kOutput, calls=%fused_computation.14 | convolution fusion | flops 100678656 | bytes 2097152 | tf_op jit(solution)/shard_map/rkb,bm->rmk/dot_general | solution.py:37
  75.2 1.8 %fusion.1 = f32[64,32,128]{2,1,0:T(8,128)S(1)} fusion(f32[32,64,128]{2,0,1:T(8,128)S(1)} %fusion.6, f32[64,128,32]{1,0,2:T(8,128)S(1)} %get-tuple-element.5), kind=kOutput, calls=%fused_computation.3 | convolution fusion | flops 100940800 | bytes 3145728 | tf_op jit(solution)/shard_map/rkb,bm->rmk/dot_general | solution.py:36
  77.0 1.3 stack.9
  78.3 1.9 %copy_dynamic-update-slice_fusion.1 = f32[2,64,16,256]{3,1,0,2:T(8,128)S(1)} fusion(f32[1,64,16,256]{3,2,1,0:T(8,128)} %stack.9), kind=kLoop, calls=%fused_computation.8 | loop fusion | bytes 2097152
  80.2 2.6 %fusion = f32[64,32,128]{2,1,0:T(8,128)} fusion(f32[32,64,128]{2,0,1:T(8,128)S(1)} %copy-done.1, f32[64,128,32]{1,0,2:T(8,128)S(1)} %get-tuple-element.5), kind=kOutput, calls=%fused_computation.1 | convolution fusion | flops 100939776 | bytes 3145728 | tf_op jit(solution)/shard_map/rkb,bm->rmk/dot_general | solution.py:39
  82.8 1.5 %stack.10 = f32[1,64,16,256]{3,2,1,0:T(8,128)S(1)} reshape(f32[64,32,128]{2,1,0:T(8,128)} %fusion) | data formatting | bytes 2097152 | tf_op jit(solution)/shard_map/stack | solution.py:40
  84.3 0.6 copy_dynamic-update-slice_fusion
  84.9 0.0 copy-start.10
  85.0 1.2 constant_dynamic-slice_fusion
  86.1 0.1 collective-permute-start
  86.3 0.1 copy.68
  86.3 0.3 mul.295
  86.7 0.1 copy.81
  86.9 0.0 copy-start.3
  86.9 0.1 collective-permute-start.1
  87.0 2.0 %collective-permute-start.2 = (f32[2,64,1,256]{3,1,0,2:T(8,128)}, f32[2,64,1,256]{3,1,0,2:T(8,128)S(1)}, u32[]{:S(2)}, u32[]{:S(2)}) collective-permute-start(f32[2,64,1,256]{3,1,0,2:T(8,128)} %get-tuple-element.19), channel_id=1, source_target_pairs={{0,3},{1,2},{2,1},{3,0},{4,7},{5,6},{6,5},{7,4},{8,11},{9,10},{10,... | collective-permute-start | bytes 393224 | tf_op jit(solution)/shard_map/ppermute | solution.py:21
  89.0 0.0 collective-permute-start.3
  89.0 1.5 %collective-permute-start.4 = (f32[2,64,1,256]{3,1,0,2:T(8,128)}, f32[2,64,1,256]{3,1,0,2:T(8,128)S(1)}, u32[]{:S(2)}, u32[]{:S(2)}) collective-permute-start(f32[2,64,1,256]{3,1,0,2:T(8,128)} %get-tuple-element.17), channel_id=1, source_target_pairs={{0,5},{1,4},{2,7},{3,6},{4,1},{5,0},{6,3},{7,2},{8,13},{9,12},{10,... | collective-permute-start | bytes 393224 | tf_op jit(solution)/shard_map/ppermute | solution.py:21
  90.5 0.1 reshape_reshape.36
  90.7 0.0 collective-permute-done
  90.7 0.1 collective-permute-start.5
  90.8 0.9 bitcast_dynamic-update-slice_fusion.14
  91.7 0.2 collective-permute-done.1
  91.9 2.8 %collective-permute-start.6 = (f32[2,64,1,256]{3,1,0,2:T(8,128)S(1)}, f32[2,64,1,256]{3,1,0,2:T(8,128)S(1)}, u32[]{:S(2)}, u32[]{:S(2)}) collective-permute-start(f32[2,64,1,256]{3,1,0,2:T(8,128)S(1)} %copy-done.8), channel_id=1, source_target_pairs={{0,7},{1,6},{2,5},{3,4},{4,3},{5,2},{6,1},{7,0},{8,15},{9,14},{10,... | collective-permute-start | bytes 393224 | tf_op jit(solution)/shard_map/ppermute | solution.py:21
  94.7 0.8 collective-permute-done.2
  95.5 1.1 collective-permute-start.7
  96.7 0.0 collective-permute-done.3
  96.7 0.0 copy-done.6
  96.7 1.0 collective-permute-start.8
  97.7 0.0 collective-permute-done.4
  97.7 0.0 copy-done.5
  97.7 1.2 collective-permute-start.9
  98.9 4.9 %collective-permute-done.5 = f32[2,64,1,256]{3,1,0,2:T(8,128)S(1)} collective-permute-done((f32[2,64,1,256]{3,1,0,2:T(8,128)S(1)}, f32[2,64,1,256]{3,1,0,2:T(8,128)S(1)}, u32[]{:S(2)}, u32[]{:S(2)}) %collective-permute-start.5) | collective-permute-done | bytes 131104 | tf_op jit(solution)/shard_map/ppermute | solution.py:21
  103.8 4.2 %collective-permute-start.10 = (f32[2,64,1,256]{3,1,0,2:T(8,128)S(1)}, f32[2,64,1,256]{3,1,0,2:T(8,128)S(1)}, u32[]{:S(2)}, u32[]{:S(2)}) collective-permute-start(f32[2,64,1,256]{3,1,0,2:T(8,128)S(1)} %copy-done.4), channel_id=1, source_target_pairs={{0,11},{1,10},{2,9},{3,8},{4,15},{5,14},{6,13},{7,12},{8,3},{9,2},... | collective-permute-start | bytes 393224 | tf_op jit(solution)/shard_map/ppermute | solution.py:21
  108.0 0.0 collective-permute-done.6
  108.0 0.4 collective-permute-start.11
  108.5 0.0 collective-permute-done.7
  108.5 0.8 collective-permute-start.12
  109.4 10.2 %collective-permute-done.8 = f32[2,64,1,256]{3,1,0,2:T(8,128)S(1)} collective-permute-done((f32[2,64,1,256]{3,1,0,2:T(8,128)S(1)}, f32[2,64,1,256]{3,1,0,2:T(8,128)S(1)}, u32[]{:S(2)}, u32[]{:S(2)}) %collective-permute-start.8) | collective-permute-done | bytes 131104 | tf_op jit(solution)/shard_map/ppermute | solution.py:21
  119.5 0.0 collective-permute-start.13
  119.6 2.9 %collective-permute-done.9 = f32[2,64,1,256]{3,1,0,2:T(8,128)S(1)} collective-permute-done((f32[2,64,1,256]{3,1,0,2:T(8,128)S(1)}, f32[2,64,1,256]{3,1,0,2:T(8,128)S(1)}, u32[]{:S(2)}, u32[]{:S(2)}) %collective-permute-start.9) | collective-permute-done | bytes 131104 | tf_op jit(solution)/shard_map/ppermute | solution.py:21
  122.5 1.0 collective-permute-start.14
  123.5 4.6 %collective-permute-done.10 = f32[2,64,1,256]{3,1,0,2:T(8,128)S(1)} collective-permute-done((f32[2,64,1,256]{3,1,0,2:T(8,128)S(1)}, f32[2,64,1,256]{3,1,0,2:T(8,128)S(1)}, u32[]{:S(2)}, u32[]{:S(2)}) %collective-permute-start.10) | collective-permute-done | bytes 131104 | tf_op jit(solution)/shard_map/ppermute | solution.py:21
  128.1 5.6 %collective-permute-done.11 = f32[2,64,1,256]{3,1,0,2:T(8,128)S(1)} collective-permute-done((f32[2,64,1,256]{3,1,0,2:T(8,128)S(1)}, f32[2,64,1,256]{3,1,0,2:T(8,128)S(1)}, u32[]{:S(2)}, u32[]{:S(2)}) %collective-permute-start.11) | collective-permute-done | bytes 131104 | tf_op jit(solution)/shard_map/ppermute | solution.py:21
  133.7 2.8 %collective-permute-done.12 = f32[2,64,1,256]{3,1,0,2:T(8,128)S(1)} collective-permute-done((f32[2,64,1,256]{3,1,0,2:T(8,128)S(1)}, f32[2,64,1,256]{3,1,0,2:T(8,128)S(1)}, u32[]{:S(2)}, u32[]{:S(2)}) %collective-permute-start.12) | collective-permute-done | bytes 131104 | tf_op jit(solution)/shard_map/ppermute | solution.py:21
  136.5 3.9 %collective-permute-done.13 = f32[2,64,1,256]{3,1,0,2:T(8,128)S(1)} collective-permute-done((f32[2,64,1,256]{3,1,0,2:T(8,128)S(1)}, f32[2,64,1,256]{3,1,0,2:T(8,128)S(1)}, u32[]{:S(2)}, u32[]{:S(2)}) %collective-permute-start.13) | collective-permute-done | bytes 131104 | tf_op jit(solution)/shard_map/ppermute | solution.py:21
  140.5 2.8 %collective-permute-done.14 = f32[2,64,1,256]{3,1,0,2:T(8,128)S(1)} collective-permute-done((f32[2,64,1,256]{3,1,0,2:T(8,128)S(1)}, f32[2,64,1,256]{3,1,0,2:T(8,128)S(1)}, u32[]{:S(2)}, u32[]{:S(2)}) %collective-permute-start.14) | collective-permute-done | bytes 131104 | tf_op jit(solution)/shard_map/ppermute | solution.py:21
  143.3 1.5 %broadcast_multiply_fusion = f32[2,1024,256]{2,1,0:T(8,128)} fusion(f32[2,1024,256]{2,1,0:T(8,128)S(1)} %bitcast_dynamic-update-slice_fusion, f32[1024,256]{1,0:T(8,128)S(1)} %bitcast.80), kind=kLoop, calls=%fused_computation.9 | loop fusion | flops 524288 | bytes 5242880 | tf_op jit(solution)/shard_map/mul | solution.py:86
  (37 shorter events, 0.2 us)
Async XLA Ops:
  3.1 6.7 %copy-start.11 = (s32[8,2]{0,1:T(2,128)S(1)}, s32[8,2]{0,1:T(2,128)}, u32[]{:S(2)}) copy-start(s32[8,2]{0,1:T(2,128)} %param.6) | copy-start | bytes 196
  3.1 6.8 %copy-start.12 = (f32[4]{0:T(128)S(1)}, f32[4]{0:T(128)}, u32[]{:S(2)}) copy-start(f32[4]{0:T(128)} %param.7) | copy-start | bytes 52
  3.1 54.1 %all-to-all-start = ((f32[2,16,64,256]{3,2,0,1:T(8,128)}), f32[2,16,64,256]{3,2,0,1:T(8,128)S(1)}, u32[]{:S(2)}, u32[]{:S(2)}) async-start(f32[2,16,64,256]{3,2,0,1:T(8,128)} %copy.55), calls=%async_computation | async-start | bytes 4194304 | tf_op jit(solution)/shard_map/all_to_all | solution.py:64
  60.3 3.5 %copy-start.2 = (f32[1,1,64,16,256]{4,2,0,3,1:T(8,128)S(1)}, f32[1,1,64,16,256]{4,2,0,3,1:T(8,128)}, u32[]{:S(2)}) copy-start(f32[1,1,64,16,256]{4,2,0,3,1:T(8,128)} %get-tuple-element.22) | copy-start | bytes 3145732
  68.3 1.3 copy-start
  78.3 1.9 %copy-start.1 = (f32[32,64,128]{2,0,1:T(8,128)S(1)}, f32[32,64,128]{2,0,1:T(8,128)}, u32[]{:S(2)}) copy-start(f32[32,64,128]{2,0,1:T(8,128)} %fusion.4) | copy-start | bytes 3145732
  84.9 1.3 copy-start.10
  86.1 4.5 %collective-permute-start = (f32[2,64,1,256]{3,1,0,2:T(8,128)}, f32[2,64,1,256]{3,1,0,2:T(8,128)}, u32[]{:S(2)}, u32[]{:S(2)}) collective-permute-start(f32[2,64,1,256]{3,1,0,2:T(8,128)} %get-tuple-element.21), channel_id=1, source_target_pairs={{0,1},{1,0},{2,3},{3,2},{4,5},{5,4},{6,7},{7,6},{8,9},{9,8},{10,11... | collective-permute-start | bytes 393224 | tf_op jit(solution)/shard_map/ppermute | solution.py:21
  86.9 3.8 %copy-start.9 = (f32[2,64,1,256]{3,1,0,2:T(8,128)S(1)}, f32[2,64,1,256]{3,1,0,2:T(8,128)}, u32[]{:S(2)}) copy-start(f32[2,64,1,256]{3,1,0,2:T(8,128)} %get-tuple-element.16) | copy-start | bytes 393220
  86.9 5.0 %copy-start.8 = (f32[2,64,1,256]{3,1,0,2:T(8,128)S(1)}, f32[2,64,1,256]{3,1,0,2:T(8,128)}, u32[]{:S(2)}) copy-start(f32[2,64,1,256]{3,1,0,2:T(8,128)} %get-tuple-element.15) | copy-start | bytes 393220
  86.9 8.7 %copy-start.7 = (f32[2,64,1,256]{3,1,0,2:T(8,128)S(1)}, f32[2,64,1,256]{3,1,0,2:T(8,128)}, u32[]{:S(2)}) copy-start(f32[2,64,1,256]{3,1,0,2:T(8,128)} %get-tuple-element.14) | copy-start | bytes 393220
  86.9 9.8 %copy-start.6 = (f32[2,64,1,256]{3,1,0,2:T(8,128)S(1)}, f32[2,64,1,256]{3,1,0,2:T(8,128)}, u32[]{:S(2)}) copy-start(f32[2,64,1,256]{3,1,0,2:T(8,128)} %get-tuple-element.13) | copy-start | bytes 393220
  86.9 10.8 %copy-start.5 = (f32[2,64,1,256]{3,1,0,2:T(8,128)S(1)}, f32[2,64,1,256]{3,1,0,2:T(8,128)}, u32[]{:S(2)}) copy-start(f32[2,64,1,256]{3,1,0,2:T(8,128)} %get-tuple-element.12) | copy-start | bytes 393220
  86.9 16.9 %copy-start.4 = (f32[2,64,1,256]{3,1,0,2:T(8,128)S(1)}, f32[2,64,1,256]{3,1,0,2:T(8,128)}, u32[]{:S(2)}) copy-start(f32[2,64,1,256]{3,1,0,2:T(8,128)} %get-tuple-element.11) | copy-start | bytes 393220
  86.9 21.1 %copy-start.3 = (f32[2,64,1,256]{3,1,0,2:T(8,128)S(1)}, f32[2,64,1,256]{3,1,0,2:T(8,128)}, u32[]{:S(2)}) copy-start(f32[2,64,1,256]{3,1,0,2:T(8,128)} %get-tuple-element.10) | copy-start | bytes 393220
  86.9 4.9 %collective-permute-start.1 = (f32[2,64,1,256]{3,1,0,2:T(8,128)}, f32[2,64,1,256]{3,1,0,2:T(8,128)S(1)}, u32[]{:S(2)}, u32[]{:S(2)}) collective-permute-start(f32[2,64,1,256]{3,1,0,2:T(8,128)} %get-tuple-element.20), channel_id=1, source_target_pairs={{0,2},{1,3},{2,0},{3,1},{4,6},{5,7},{6,4},{7,5},{8,10},{9,11},{10,... | collective-permute-start | bytes 393224 | tf_op jit(solution)/shard_map/ppermute | solution.py:21
  87.0 8.5 %collective-permute-start.2 = (f32[2,64,1,256]{3,1,0,2:T(8,128)}, f32[2,64,1,256]{3,1,0,2:T(8,128)S(1)}, u32[]{:S(2)}, u32[]{:S(2)}) collective-permute-start(f32[2,64,1,256]{3,1,0,2:T(8,128)} %get-tuple-element.19), channel_id=1, source_target_pairs={{0,3},{1,2},{2,1},{3,0},{4,7},{5,6},{6,5},{7,4},{8,11},{9,10},{10,... | collective-permute-start | bytes 393224 | tf_op jit(solution)/shard_map/ppermute | solution.py:21
  89.0 7.7 %collective-permute-start.3 = (f32[2,64,1,256]{3,1,0,2:T(8,128)}, f32[2,64,1,256]{3,1,0,2:T(8,128)S(1)}, u32[]{:S(2)}, u32[]{:S(2)}) collective-permute-start(f32[2,64,1,256]{3,1,0,2:T(8,128)} %get-tuple-element.18), channel_id=1, source_target_pairs={{0,4},{1,5},{2,6},{3,7},{4,0},{5,1},{6,2},{7,3},{8,12},{9,13},{10,... | collective-permute-start | bytes 393224 | tf_op jit(solution)/shard_map/ppermute | solution.py:21
  89.0 8.7 %collective-permute-start.4 = (f32[2,64,1,256]{3,1,0,2:T(8,128)}, f32[2,64,1,256]{3,1,0,2:T(8,128)S(1)}, u32[]{:S(2)}, u32[]{:S(2)}) collective-permute-start(f32[2,64,1,256]{3,1,0,2:T(8,128)} %get-tuple-element.17), channel_id=1, source_target_pairs={{0,5},{1,4},{2,7},{3,6},{4,1},{5,0},{6,3},{7,2},{8,13},{9,12},{10,... | collective-permute-start | bytes 393224 | tf_op jit(solution)/shard_map/ppermute | solution.py:21
  90.7 13.1 %collective-permute-start.5 = (f32[2,64,1,256]{3,1,0,2:T(8,128)S(1)}, f32[2,64,1,256]{3,1,0,2:T(8,128)S(1)}, u32[]{:S(2)}, u32[]{:S(2)}) collective-permute-start(f32[2,64,1,256]{3,1,0,2:T(8,128)S(1)} %copy-done.9), channel_id=1, source_target_pairs={{0,6},{1,7},{2,4},{3,5},{4,2},{5,3},{6,0},{7,1},{8,14},{9,15},{10,... | collective-permute-start | bytes 393224 | tf_op jit(solution)/shard_map/ppermute | solution.py:21
  91.9 16.2 %collective-permute-start.6 = (f32[2,64,1,256]{3,1,0,2:T(8,128)S(1)}, f32[2,64,1,256]{3,1,0,2:T(8,128)S(1)}, u32[]{:S(2)}, u32[]{:S(2)}) collective-permute-start(f32[2,64,1,256]{3,1,0,2:T(8,128)S(1)} %copy-done.8), channel_id=1, source_target_pairs={{0,7},{1,6},{2,5},{3,4},{4,3},{5,2},{6,1},{7,0},{8,15},{9,14},{10,... | collective-permute-start | bytes 393224 | tf_op jit(solution)/shard_map/ppermute | solution.py:21
  95.5 13.0 %collective-permute-start.7 = (f32[2,64,1,256]{3,1,0,2:T(8,128)S(1)}, f32[2,64,1,256]{3,1,0,2:T(8,128)S(1)}, u32[]{:S(2)}, u32[]{:S(2)}) collective-permute-start(f32[2,64,1,256]{3,1,0,2:T(8,128)S(1)} %copy-done.7), channel_id=1, source_target_pairs={{0,8},{1,9},{2,10},{3,11},{4,12},{5,13},{6,14},{7,15},{8,0},{9,1},... | collective-permute-start | bytes 393224 | tf_op jit(solution)/shard_map/ppermute | solution.py:21
  96.7 22.8 %collective-permute-start.8 = (f32[2,64,1,256]{3,1,0,2:T(8,128)S(1)}, f32[2,64,1,256]{3,1,0,2:T(8,128)S(1)}, u32[]{:S(2)}, u32[]{:S(2)}) collective-permute-start(f32[2,64,1,256]{3,1,0,2:T(8,128)S(1)} %copy-done.6), channel_id=1, source_target_pairs={{0,9},{1,8},{2,11},{3,10},{4,13},{5,12},{6,15},{7,14},{8,1},{9,0},... | collective-permute-start | bytes 393224 | tf_op jit(solution)/shard_map/ppermute | solution.py:21
  97.7 24.8 %collective-permute-start.9 = (f32[2,64,1,256]{3,1,0,2:T(8,128)S(1)}, f32[2,64,1,256]{3,1,0,2:T(8,128)S(1)}, u32[]{:S(2)}, u32[]{:S(2)}) collective-permute-start(f32[2,64,1,256]{3,1,0,2:T(8,128)S(1)} %copy-done.5), channel_id=1, source_target_pairs={{0,10},{1,11},{2,8},{3,9},{4,14},{5,15},{6,12},{7,13},{8,2},{9,3},... | collective-permute-start | bytes 393224 | tf_op jit(solution)/shard_map/ppermute | solution.py:21
  103.8 24.3 %collective-permute-start.10 = (f32[2,64,1,256]{3,1,0,2:T(8,128)S(1)}, f32[2,64,1,256]{3,1,0,2:T(8,128)S(1)}, u32[]{:S(2)}, u32[]{:S(2)}) collective-permute-start(f32[2,64,1,256]{3,1,0,2:T(8,128)S(1)} %copy-done.4), channel_id=1, source_target_pairs={{0,11},{1,10},{2,9},{3,8},{4,15},{5,14},{6,13},{7,12},{8,3},{9,2},... | collective-permute-start | bytes 393224 | tf_op jit(solution)/shard_map/ppermute | solution.py:21
  108.0 25.7 %collective-permute-start.11 = (f32[2,64,1,256]{3,1,0,2:T(8,128)S(1)}, f32[2,64,1,256]{3,1,0,2:T(8,128)S(1)}, u32[]{:S(2)}, u32[]{:S(2)}) collective-permute-start(f32[2,64,1,256]{3,1,0,2:T(8,128)S(1)} %copy-done.3), channel_id=1, source_target_pairs={{0,12},{1,13},{2,14},{3,15},{4,8},{5,9},{6,10},{7,11},{8,4},{9,5},... | collective-permute-start | bytes 393224 | tf_op jit(solution)/shard_map/ppermute | solution.py:21
  108.5 28.0 %collective-permute-start.12 = (f32[2,64,1,256]{3,1,0,2:T(8,128)S(1)}, f32[2,64,1,256]{3,1,0,2:T(8,128)S(1)}, u32[]{:S(2)}, u32[]{:S(2)}) collective-permute-start(f32[2,64,1,256]{3,1,0,2:T(8,128)S(1)} %get-tuple-element.9), channel_id=1, source_target_pairs={{0,13},{1,12},{2,15},{3,14},{4,9},{5,8},{6,11},{7,10},{8,5},{9,4},... | collective-permute-start | bytes 393224 | tf_op jit(solution)/shard_map/ppermute | solution.py:21
  119.5 20.9 %collective-permute-start.13 = (f32[2,64,1,256]{3,1,0,2:T(8,128)S(1)}, f32[2,64,1,256]{3,1,0,2:T(8,128)S(1)}, u32[]{:S(2)}, u32[]{:S(2)}) collective-permute-start(f32[2,64,1,256]{3,1,0,2:T(8,128)S(1)} %get-tuple-element.8), channel_id=1, source_target_pairs={{0,14},{1,15},{2,12},{3,13},{4,10},{5,11},{6,8},{7,9},{8,6},{9,7},... | collective-permute-start | bytes 393224 | tf_op jit(solution)/shard_map/ppermute | solution.py:21
  122.5 20.8 %collective-permute-start.14 = (f32[2,64,1,256]{3,1,0,2:T(8,128)S(1)}, f32[2,64,1,256]{3,1,0,2:T(8,128)S(1)}, u32[]{:S(2)}, u32[]{:S(2)}) collective-permute-start(f32[2,64,1,256]{3,1,0,2:T(8,128)S(1)} %get-tuple-element.7), channel_id=1, source_target_pairs={{0,15},{1,14},{2,13},{3,12},{4,11},{5,10},{6,9},{7,8},{8,7},{9,6},... | collective-permute-start | bytes 393224 | tf_op jit(solution)/shard_map/ppermute | solution.py:21
